TPU v7x, 32 devices: a whole 2x2x4 slice. The times are simulated.
32 devices in a mesh: layer: 4 (over x, core), dp: 8 (over z, y).
Axes of the slice: x: 2, y: 2, z: 4, core: 2. Of those that a mesh axis runs over, the one named last changes fastest.
Arguments:
- out_grads: bfloat16 [4, 128, 16384], P('layer', None, 'dp'), may hold values from -3 to 3
- in_acts: bfloat16 [4, 128, 4096], P('layer', None, 'dp'), may hold values from -3 to 3
- out_basis: bfloat16 [4, 16384, 16384], P('layer', None, 'dp'), may hold values from -0.046875 to 0.046875
- in_basis: bfloat16 [4, 4096, 4096], P('layer', None, 'dp'), may hold values from -0.09375 to 0.09375
- eigenvalues: bfloat16 [4, 16384, 4096], P('layer', 'dp'), may hold values from 0.5 to 50
- out_store: bfloat16 [4, 16, 32, 16384], P('layer', 'dp'), may hold values from -0.046875 to 0.046875
- in_store: bfloat16 [4, 16, 32, 4096], P('layer', 'dp'), may hold values from -0.09375 to 0.09375
- counts: int32 [16], P('dp'), may hold values from 1 to 4096
- winners: int32 [4, 6], replicated, may hold values from 0 to 15
Outputs:
- influence: float32 [4, 6, 32], replicated
All inputs are finite; a program needn't handle non-finite values.
Results may differ from a plain program's by a relative error of at most 0.0055.
Values may be sent and summed in bfloat16 or wider, within the bound.
A program may use at most 192 MiB of HBM per device.

v0:
```python
import jax
import jax.numpy as jnp
from jax import lax
from jax.sharding import PartitionSpec as P

NQ = 4
TQ = 32
WIN = 6
R = 32
SPAN = 128
damping = 0.1


def on_device(
    out_grads, in_acts, out_basis, in_basis, eigenvalues, out_store, in_store, counts, winners
):
    out_local = out_basis[0]
    in_local = in_basis[0]
    out_width = out_local.shape[1]
    rows = out_local
    turned_out = jnp.dot(
        lax.all_gather(out_grads[0], "dp", axis=1, tiled=True),
        rows,
        preferred_element_type=jnp.float32,
    ).astype(jnp.bfloat16)
    rows = in_local
    turned_part = jnp.dot(
        lax.all_gather(in_acts[0], "dp", axis=1, tiled=True),
        rows,
        preferred_element_type=jnp.float32,
    ).astype(jnp.bfloat16)
    turned_in = lax.all_gather(turned_part, "dp", axis=1, tiled=True)
    left = turned_out.reshape(NQ, TQ, out_width)
    right = turned_in.reshape(NQ, TQ, turned_in.shape[1])
    product = jnp.einsum("qtf,qtd->qfd", left, right, preferred_element_type=jnp.float32)
    divisor = eigenvalues[0].astype(jnp.float32) + damping
    precond = (product / divisor[None]).astype(jnp.bfloat16)
    alive = (jnp.arange(R, dtype=jnp.int32)[None, :] * SPAN < counts[:, None]).astype(jnp.bfloat16)
    masked = in_store[0] * alive[:, :, None]
    out_slices = lax.all_to_all(out_store[0], "dp", split_axis=2, concat_axis=0, tiled=True)
    chosen = winners.reshape(NQ * WIN)
    left_rows = jnp.take(out_slices, chosen, axis=0).reshape(NQ, WIN * R, out_width)
    full_width = turned_in.shape[1]
    in_whole = lax.all_gather(masked, "dp", axis=0, tiled=True)
    right_rows = jnp.take(in_whole, chosen, axis=0).reshape(NQ, WIN * R, full_width)
    mapped = jnp.einsum("qfd,qkd->qkf", precond, right_rows, preferred_element_type=jnp.float32)
    partial_value = jnp.sum(mapped * left_rows.astype(jnp.float32), axis=2)
    totals = lax.psum(partial_value, ("layer", "dp"))
    return totals.reshape(NQ, WIN, R)


def solution(mesh):
    placed = (
        P("layer", None, "dp"),
        P("layer", None, "dp"),
        P("layer", None, "dp"),
        P("layer", None, "dp"),
        P("layer", "dp", None),
        P("layer", "dp", None, None),
        P("layer", "dp", None, None),
        P("dp"),
        P(),
    )
    return jax.shard_map(on_device, mesh=mesh, in_specs=placed, out_specs=P(), check_vma=False)
```

profile of v0, /device:TPU:0, one launch (start us, length us, event | category | flops | bytes accessed | tf_op | source)
XLA Modules:
  0.0 364.3 jit_solution(16281501123913025915)
XLA Ops:
  6.5 0.0 all-gather.13.cloned.1.call-start
  6.5 0.7 all-gather.13.cloned.1.call-update
  7.3 0.0 all-gather.11.cloned.1.call-start
  7.3 0.7 all-gather.11.cloned.1.call-update
  8.0 0.0 all-gather.7.cloned.1.call-start
  8.1 0.7 compare_convert_fusion
  8.8 2.0 bitcast_multiply_fusion
  10.7 0.0 all-gather.7.cloned.1.call-update
  10.8 17.2 %copy.13 = bf16[1,2,32,16384]{2,1,3,0:T(2,128)(2,1)} copy(bf16[1,2,32,16384]{3,2,1,0:T(8,128)(2,1)} %param.14) | data formatting | bytes 4194304 | tf_op args[5]
  28.0 8.0 %bitcast_bitcast_fusion = bf16[16384,2,32]{2,1,0:T(2,128)(2,1)} fusion(bf16[1,2,32,16384]{2,1,3,0:T(2,128)(2,1)} %copy.13), kind=kLoop, calls=%fused_computation.25 | loop fusion | bytes 4194304
  36.0 0.0 copy-start.1
  36.0 11.2 %reshape.112 = bf16[8,2,65536]{2,1,0:T(2,128)(2,1)} reshape(bf16[16384,2,32]{2,1,0:T(2,128)(2,1)} %bitcast_bitcast_fusion) | data formatting | bytes 4194304
  47.2 7.3 %all-to-all-start = ((bf16[8,2,65536]{2,1,0:T(2,128)(2,1)}), bf16[8,2,65536]{2,1,0:T(2,128)(2,1)S(1)}, u32[]{:S(2)}, u32[]{:S(2)}) async-start(bf16[8,2,65536]{2,1,0:T(2,128)(2,1)} %reshape.112), calls=%async_computation | async-start | bytes 4194304 | tf_op jit(solution)/shard_map/all_to_all | solution.py:40
  54.5 0.0 all-gather.9.cloned.1.call-start
  54.6 0.0 copy-done.1
  54.6 0.1 reshape.90
  54.7 0.1 broadcast_in_dim.28
  54.8 0.1 broadcast_in_dim.29
  54.9 18.8 %add_bitcast_fusion = f32[2048,4096]{1,0:T(8,128)} fusion(bf16[1,2048,4096]{2,1,0:T(8,128)(2,1)} %param.13), kind=kLoop, calls=%fused_computation.6 | loop fusion | flops 16777216 | bytes 50331648 | tf_op jit(solution)/shard_map/div | solution.py:37
  73.7 0.0 all-gather.13.cloned.1.call-done
  73.7 3.9 %fusion.13 = bf16[128,512]{1,0:T(8,128)(2,1)} fusion(bf16[1,4096,512]{2,1,0:T(8,128)(2,1)} %param.12, bf16[1,128,4096]{2,1,0:T(8,128)(2,1)} %all-gather.13.cloned.1.call-done), kind=kOutput, calls=%fused_computation.15 | convolution fusion | flops 536936448 | bytes 5373952 | tf_op jit(solution)/shard_map/dot_general | solution.py:27
  77.6 0.0 all-gather.9.cloned.1.call-update
  77.6 50.9 %all-to-all-done = bf16[8,2,65536]{2,1,0:T(2,128)(2,1)S(1)} async-done(((bf16[8,2,65536]{2,1,0:T(2,128)(2,1)}), bf16[8,2,65536]{2,1,0:T(2,128)(2,1)S(1)}, u32[]{:S(2)}, u32[]{:S(2)}) %all-to-all-start) | async-done | bytes 2097184 | tf_op jit(solution)/shard_map/all_to_all | solution.py:40
  128.5 6.5 %reshape.113 = bf16[16384,2,32]{2,1,0:T(2,128)(2,1)} reshape(bf16[8,2,65536]{2,1,0:T(2,128)(2,1)S(1)} %all-to-all-done) | data formatting | bytes 4194304
  135.0 17.8 %copy.18 = bf16[2,32,8,2048]{3,1,0,2:T(8,128)(2,1)S(1)} copy(bf16[2,32,8,2048]{1,0,3,2:T(2,128)(2,1)} %bitcast.47) | data formatting | bytes 4194304 | tf_op jit(solution)/shard_map/all_to_all | solution.py:40
  152.8 2.5 gather_fusion.1
  155.3 0.0 all-gather.11.cloned.1.call-done
  155.3 26.3 %fusion.8 = bf16[128,2048]{1,0:T(8,128)(2,1)} fusion(bf16[1,16384,2048]{2,1,0:T(8,128)(2,1)} %param.11, bf16[1,128,16384]{2,1,0:T(8,128)(2,1)} %all-gather.11.cloned.1.call-done), kind=kOutput, calls=%fused_computation.14 | convolution fusion | flops 8590196736 | bytes 71827456 | tf_op jit(solution)/shard_map/dot_general | solution.py:21
  181.5 46.3 %all-gather.7.cloned.1.call-done = bf16[16,32,4096]{2,1,0:T(8,128)(2,1)} async-done(((bf16[2,32,4096]{2,1,0:T(8,128)(2,1)}), bf16[16,32,4096]{2,1,0:T(8,128)(2,1)}) %all-gather.7.cloned.1.call-update) | async-done | bytes 4194320 | tf_op jit(solution)/shard_map/all_gather | solution.py:44
  227.8 6.5 %gather_fusion = bf16[24,32,4096]{2,1,0:T(8,128)(2,1)} fusion(bf16[16,32,4096]{2,1,0:T(8,128)(2,1)} %all-gather.7.cloned.1.call-done, s32[1024]{0:T(1024)S(1)} %pad_clamp_fusion), kind=kCustom, calls=%fused_computation | custom fusion | bytes 12583008 | tf_op jit(solution)/shard_map/jit(_take)/gather | solution.py:45
  234.3 6.1 %bitcast_select_fusion = bf16[4,192,4096]{2,1,0:T(8,128)(2,1)} fusion(pred[4,192]{1,0:T(4,128)(4,1)S(1)} %broadcast_in_dim.29, bf16[4,192,4096]{2,1,0:T(8,128)(2,1)} %bitcast.48), kind=kLoop, calls=%fused_computation.8 | loop fusion | flops 3145728 | bytes 12583680 | tf_op jit(solution)/shard_map/jit(_take)/select_n | solution.py:45
  240.5 27.2 %all-gather.9.cloned.1.call-done = bf16[128,4096]{1,0:T(8,128)(2,1)} async-done(((bf16[128,512]{1,0:T(8,128)(2,1)}), bf16[128,4096]{1,0:T(8,128)(2,1)}) %all-gather.9.cloned.1.call-update) | async-done | bytes 1048592 | tf_op jit(solution)/shard_map/all_gather | solution.py:32
  267.7 0.0 copy-start
  267.7 45.8 %fusion.2 = f32[4,192,2048]{2,1,0:T(8,128)} fusion(bf16[4,192,4096]{2,1,0:T(8,128)(2,1)} %bitcast_select_fusion, f32[2048,4096]{1,0:T(8,128)} %add_bitcast_fusion, bf16[4,32,2048]{2,1,0:T(8,128)(2,1)} %bitcast.51, bf16[4,32,4096]{2,1,0:T(8,128)(2,1)} %bitcast.52), kind=kOutput, calls=%fused_computation.5 | convolution fusion | flops 15099494400 | bytes 47710208 | tf_op jit(solution)/shard_map/qfd,qkd->qkf/dot_general | solution.py:46
  313.5 0.0 copy-done
  313.5 3.8 %multiply_reduce_fusion = f32[4,192]{1,0:T(4,128)S(1)} fusion(f32[4,192,2048]{2,1,0:T(8,128)} %fusion.2, pred[4,192]{1,0:T(4,128)(4,1)S(1)} %broadcast_in_dim.29, bf16[4,192,2048]{2,1,0:T(8,128)(2,1)S(1)} %bitcast.50), kind=kLoop, calls=%fused_computation.9 | loop fusion | flops 6290688 | bytes 9441024 | tf_op jit(solution)/shard_map/reduce_sum | solution.py:47
  317.3 0.1 reshape.93
  317.4 39.8 %psum.7 = f32[4,6,32]{2,1,0:T(8,128)S(1)} all-reduce(f32[4,6,32]{2,1,0:T(8,128)S(1)} %reshape.93), channel_id=1, replica_groups=mesh['layer'=4,'dp'=8] {'layer','dp'}, use_global_device_ids=true, to_apply=%region_1.2 | all-reduce | flops 768 | bytes 6144 | tf_op jit(solution)/shard_map/psum | solution.py:48
  357.2 0.6 copy.16
  (4 shorter events, 0.0 us)
Async XLA Ops:
  6.5 67.1 %all-gather.13.cloned.1.call-start = ((), (), s32[]{:S(2)}) async-start(), calls=%async_computation.4 | async-start | bytes 1179648 | tf_op jit(solution)/shard_map/all_gather | solution.py:28
  7.3 148.0 %all-gather.11.cloned.1.call-start = ((), (), s32[]{:S(2)}) async-start(), calls=%async_computation.3 | async-start | bytes 4718592 | tf_op jit(solution)/shard_map/all_gather | solution.py:22
  8.0 219.8 %all-gather.7.cloned.1.call-start = ((), (), s32[]{:S(2)}) async-start(), calls=%async_computation.1 | async-start | bytes 4718592 | tf_op jit(solution)/shard_map/all_gather | solution.py:44
  36.0 18.6 %copy-start.1 = (s32[4,6]{1,0:T(4,128)S(1)}, s32[4,6]{1,0:T(4,128)}, u32[]{:S(2)}) copy-start(s32[4,6]{1,0:T(4,128)} %param.17) | copy-start | bytes 292
  47.2 81.3 %all-to-all-start = ((bf16[8,2,65536]{2,1,0:T(2,128)(2,1)}), bf16[8,2,65536]{2,1,0:T(2,128)(2,1)S(1)}, u32[]{:S(2)}, u32[]{:S(2)}) async-start(bf16[8,2,65536]{2,1,0:T(2,128)(2,1)} %reshape.112), calls=%async_computation | async-start | bytes 4194304 | tf_op jit(solution)/shard_map/all_to_all | solution.py:40
  54.5 213.1 %all-gather.9.cloned.1.call-start = ((), (), s32[]{:S(2)}) async-start(), calls=%async_computation.2 | async-start | bytes 1179648 | tf_op jit(solution)/shard_map/all_gather | solution.py:32
  267.7 45.8 %copy-start = (bf16[24,32,2048]{2,1,0:T(8,128)(2,1)S(1)}, bf16[24,32,2048]{2,1,0:T(8,128)(2,1)}, u32[]{:S(2)}) copy-start(bf16[24,32,2048]{2,1,0:T(8,128)(2,1)} %gather_fusion.1) | copy-start | bytes 9437188
Sparse Core Ops, SparseCore 0:
  9.4 42.1 all-gather.12
  53.7 100.1 all-gather.10
  156.0 71.7 all-gather.6
  229.7 37.9 all-gather.8
where the time goes:
time: 366 us; the launch traced here: 364 us
  waiting for transfers between devices  126 us (34%)
  matrix products  76 us (21%)
  local copies, waits for them, and re-layouts  70.7 us (19%)
  blocking collectives  39.8 us (11%)
  other arithmetic  31.4 us (9%)
  between operations  13.2 us (4%)
  starting transfers between devices  7.43 us (2%)
    all_to_all x1, waiting for transfers between devices, on_device(): lax.all_to_all(out_store[0], 'dp', split_axis=2, concat_axis=0, tiled=True)  50.9 us
    all_gather x1, waiting for transfers between devices, on_device(): in_whole = lax.all_gather(masked, 'dp', axis=0, tiled=True)  46.3 us
    dot_general x1, matrix products, on_device(): jnp.einsum('qfd,qkd->qkf', precond, right_rows, preferred_element_type=jn...  45.8 us
    unnamed x8, local copies, waits for them, and re-layouts  43 us
    psum x1, blocking collectives, on_device(): totals = lax.psum(partial_value, ('layer', 'dp'))  39.8 us
    all_gather x1, waiting for transfers between devices, on_device(): turned_in = lax.all_gather(turned_part, 'dp', axis=1, tiled=True)  27.2 us
    dot_general x1, matrix products, on_device(): jnp.dot(lax.all_gather(out_grads[0], 'dp', axis=1, tiled=True), rows, pre...  26.3 us
    div x1, other arithmetic, on_device(): precond = (product / divisor[None]).astype(jnp.bfloat16)  18.8 us
  transfers between devices with their start and end apart: 5, of which 3 were waited for; matrix products, arithmetic and copies ran while one was open for 35% of the time, Pallas kernels for 0%

commit v1 on v0

--- a/solution.py
+++ b/solution.py
@@ -45,7 +45,7 @@
     right_rows = jnp.take(in_whole, chosen, axis=0).reshape(NQ, WIN * R, full_width)
     mapped = jnp.einsum("qfd,qkd->qkf", precond, right_rows, preferred_element_type=jnp.float32)
     partial_value = jnp.sum(mapped * left_rows.astype(jnp.float32), axis=2)
-    totals = lax.psum(partial_value, ("layer", "dp"))
+    totals = lax.psum(lax.psum(partial_value, "dp"), "layer")
     return totals.reshape(NQ, WIN, R)
 
 

time: 366 us -> 356 us (0.973)
  blocking collectives: 39.8 us -> 29.3 us
    psum x1 -> x2, blocking collectives: 39.8 us -> 29.3 us  [on_device(): totals = lax.psum(lax.psum(partial_value, 'dp'), 'layer')]
  transfers between devices with their start and end apart: 5 -> 5, of which waited for: 3 -> 3; matrix products, arithmetic and copies ran while one was open for 35% -> 36% of each run, Pallas kernels for 0% -> 0%
where the time goes in v1:
time: 356 us; the launch traced here: 354 us
  waiting for transfers between devices  126 us (35%)
  matrix products  76 us (21%)
  local copies, waits for them, and re-layouts  70.6 us (20%)
  other arithmetic  31.3 us (9%)
  blocking collectives  29.3 us (8%)
  between operations  13.2 us (4%)
  starting transfers between devices  7.43 us (2%)
    all_to_all x1, waiting for transfers between devices, on_device(): lax.all_to_all(out_store[0], 'dp', split_axis=2, concat_axis=0, tiled=True)  50.9 us
    all_gather x1, waiting for transfers between devices, on_device(): in_whole = lax.all_gather(masked, 'dp', axis=0, tiled=True)  46.3 us
    dot_general x1, matrix products, on_device(): jnp.einsum('qfd,qkd->qkf', precond, right_rows, preferred_element_type=jn...  45.8 us
    unnamed x8, local copies, waits for them, and re-layouts  42.9 us
    psum x2, blocking collectives, on_device(): totals = lax.psum(lax.psum(partial_value, 'dp'), 'layer')  29.3 us
    all_gather x1, waiting for transfers between devices, on_device(): turned_in = lax.all_gather(turned_part, 'dp', axis=1, tiled=True)  27.2 us
    dot_general x1, matrix products, on_device(): jnp.dot(lax.all_gather(out_grads[0], 'dp', axis=1, tiled=True), rows, pre...  26.3 us
    div x1, other arithmetic, on_device(): precond = (product / divisor[None]).astype(jnp.bfloat16)  18.7 us
  transfers between devices with their start and end apart: 5, of which 3 were waited for; matrix products, arithmetic and copies ran while one was open for 36% of the time, Pallas kernels for 0%

profile of v1, /device:TPU:0, one launch (start us, length us, event | category | flops | bytes accessed | tf_op | source)
XLA Modules:
  0.0 353.8 jit_solution(13576207420941662481)
XLA Ops:
  6.5 0.0 all-gather.13.cloned.1.call-start
  6.5 0.7 all-gather.13.cloned.1.call-update
  7.3 0.0 all-gather.11.cloned.1.call-start
  7.3 0.7 all-gather.11.cloned.1.call-update
  8.0 0.0 all-gather.7.cloned.1.call-start
  8.1 0.7 compare_convert_fusion
  8.8 2.0 bitcast_multiply_fusion
  10.8 0.0 all-gather.7.cloned.1.call-update
  10.8 17.2 %copy.13 = bf16[1,2,32,16384]{2,1,3,0:T(2,128)(2,1)} copy(bf16[1,2,32,16384]{3,2,1,0:T(8,128)(2,1)} %param.14) | data formatting | bytes 4194304 | tf_op args[5]
  28.0 8.0 %bitcast_bitcast_fusion = bf16[16384,2,32]{2,1,0:T(2,128)(2,1)} fusion(bf16[1,2,32,16384]{2,1,3,0:T(2,128)(2,1)} %copy.13), kind=kLoop, calls=%fused_computation.25 | loop fusion | bytes 4194304
  36.0 0.0 copy-start.1
  36.0 11.2 %reshape.112 = bf16[8,2,65536]{2,1,0:T(2,128)(2,1)} reshape(bf16[16384,2,32]{2,1,0:T(2,128)(2,1)} %bitcast_bitcast_fusion) | data formatting | bytes 4194304
  47.2 7.3 %all-to-all-start = ((bf16[8,2,65536]{2,1,0:T(2,128)(2,1)}), bf16[8,2,65536]{2,1,0:T(2,128)(2,1)S(1)}, u32[]{:S(2)}, u32[]{:S(2)}) async-start(bf16[8,2,65536]{2,1,0:T(2,128)(2,1)} %reshape.112), calls=%async_computation | async-start | bytes 4194304 | tf_op jit(solution)/shard_map/all_to_all | solution.py:40
  54.5 0.0 all-gather.9.cloned.1.call-start
  54.6 0.0 copy-done.1
  54.6 0.1 reshape.90
  54.7 0.1 broadcast_in_dim.28
  54.8 0.1 broadcast_in_dim.29
  54.9 18.7 %add_bitcast_fusion = f32[2048,4096]{1,0:T(8,128)} fusion(bf16[1,2048,4096]{2,1,0:T(8,128)(2,1)} %param.13), kind=kLoop, calls=%fused_computation.6 | loop fusion | flops 16777216 | bytes 50331648 | tf_op jit(solution)/shard_map/div | solution.py:37
  73.6 0.0 all-gather.13.cloned.1.call-done
  73.6 3.9 %fusion.13 = bf16[128,512]{1,0:T(8,128)(2,1)} fusion(bf16[1,4096,512]{2,1,0:T(8,128)(2,1)} %param.12, bf16[1,128,4096]{2,1,0:T(8,128)(2,1)} %all-gather.13.cloned.1.call-done), kind=kOutput, calls=%fused_computation.15 | convolution fusion | flops 536936448 | bytes 5373952 | tf_op jit(solution)/shard_map/dot_general | solution.py:27
  77.5 0.0 all-gather.9.cloned.1.call-update
  77.5 50.9 %all-to-all-done = bf16[8,2,65536]{2,1,0:T(2,128)(2,1)S(1)} async-done(((bf16[8,2,65536]{2,1,0:T(2,128)(2,1)}), bf16[8,2,65536]{2,1,0:T(2,128)(2,1)S(1)}, u32[]{:S(2)}, u32[]{:S(2)}) %all-to-all-start) | async-done | bytes 2097184 | tf_op jit(solution)/shard_map/all_to_all | solution.py:40
  128.5 6.5 %reshape.113 = bf16[16384,2,32]{2,1,0:T(2,128)(2,1)} reshape(bf16[8,2,65536]{2,1,0:T(2,128)(2,1)S(1)} %all-to-all-done) | data formatting | bytes 4194304
  135.0 17.8 %copy.18 = bf16[2,32,8,2048]{3,1,0,2:T(8,128)(2,1)S(1)} copy(bf16[2,32,8,2048]{1,0,3,2:T(2,128)(2,1)} %bitcast.47) | data formatting | bytes 4194304 | tf_op jit(solution)/shard_map/all_to_all | solution.py:40
  152.8 2.5 gather_fusion.1
  155.2 0.0 all-gather.11.cloned.1.call-done
  155.2 26.3 %fusion.8 = bf16[128,2048]{1,0:T(8,128)(2,1)} fusion(bf16[1,16384,2048]{2,1,0:T(8,128)(2,1)} %param.11, bf16[1,128,16384]{2,1,0:T(8,128)(2,1)} %all-gather.11.cloned.1.call-done), kind=kOutput, calls=%fused_computation.14 | convolution fusion | flops 8590196736 | bytes 71827456 | tf_op jit(solution)/shard_map/dot_general | solution.py:21
  181.5 46.3 %all-gather.7.cloned.1.call-done = bf16[16,32,4096]{2,1,0:T(8,128)(2,1)} async-done(((bf16[2,32,4096]{2,1,0:T(8,128)(2,1)}), bf16[16,32,4096]{2,1,0:T(8,128)(2,1)}) %all-gather.7.cloned.1.call-update) | async-done | bytes 4194320 | tf_op jit(solution)/shard_map/all_gather | solution.py:44
  227.8 6.5 %gather_fusion = bf16[24,32,4096]{2,1,0:T(8,128)(2,1)} fusion(bf16[16,32,4096]{2,1,0:T(8,128)(2,1)} %all-gather.7.cloned.1.call-done, s32[1024]{0:T(1024)S(1)} %pad_clamp_fusion), kind=kCustom, calls=%fused_computation | custom fusion | bytes 12583008 | tf_op jit(solution)/shard_map/jit(_take)/gather | solution.py:45
  234.3 6.1 %bitcast_select_fusion = bf16[4,192,4096]{2,1,0:T(8,128)(2,1)} fusion(pred[4,192]{1,0:T(4,128)(4,1)S(1)} %broadcast_in_dim.29, bf16[4,192,4096]{2,1,0:T(8,128)(2,1)} %bitcast.48), kind=kLoop, calls=%fused_computation.8 | loop fusion | flops 3145728 | bytes 12583680 | tf_op jit(solution)/shard_map/jit(_take)/select_n | solution.py:45
  240.4 27.2 %all-gather.9.cloned.1.call-done = bf16[128,4096]{1,0:T(8,128)(2,1)} async-done(((bf16[128,512]{1,0:T(8,128)(2,1)}), bf16[128,4096]{1,0:T(8,128)(2,1)}) %all-gather.9.cloned.1.call-update) | async-done | bytes 1048592 | tf_op jit(solution)/shard_map/all_gather | solution.py:32
  267.6 0.0 copy-start
  267.7 45.8 %fusion.2 = f32[4,192,2048]{2,1,0:T(8,128)} fusion(bf16[4,192,4096]{2,1,0:T(8,128)(2,1)} %bitcast_select_fusion, f32[2048,4096]{1,0:T(8,128)} %add_bitcast_fusion, bf16[4,32,2048]{2,1,0:T(8,128)(2,1)} %bitcast.51, bf16[4,32,4096]{2,1,0:T(8,128)(2,1)} %bitcast.52), kind=kOutput, calls=%fused_computation.5 | convolution fusion | flops 15099494400 | bytes 47710208 | tf_op jit(solution)/shard_map/qfd,qkd->qkf/dot_general | solution.py:46
  313.5 0.0 copy-done
  313.5 3.8 %multiply_reduce_fusion = f32[4,192]{1,0:T(4,128)S(1)} fusion(f32[4,192,2048]{2,1,0:T(8,128)} %fusion.2, pred[4,192]{1,0:T(4,128)(4,1)S(1)} %broadcast_in_dim.29, bf16[4,192,2048]{2,1,0:T(8,128)(2,1)S(1)} %bitcast.50), kind=kLoop, calls=%fused_computation.9 | loop fusion | flops 6290688 | bytes 9441024 | tf_op jit(solution)/shard_map/reduce_sum | solution.py:47
  317.2 19.2 %psum.14 = f32[4,192]{1,0:T(4,128)S(1)} all-reduce(f32[4,192]{1,0:T(4,128)S(1)} %multiply_reduce_fusion), channel_id=1, replica_groups=mesh['layer'=4,'dp'=8] {'dp'}, use_global_device_ids=true, to_apply=%region_1.2 | all-reduce | flops 768 | bytes 6144 | tf_op jit(solution)/shard_map/psum | solution.py:48
  336.5 0.1 reshape.93
  336.5 10.1 %psum.15 = f32[4,6,32]{2,1,0:T(8,128)S(1)} all-reduce(f32[4,6,32]{2,1,0:T(8,128)S(1)} %reshape.93), channel_id=1, replica_groups=mesh['layer'=4,'dp'=8] {'layer'}, use_global_device_ids=true, to_apply=%region_2.3 | all-reduce | flops 768 | bytes 6144 | tf_op jit(solution)/shard_map/psum | solution.py:48
  346.6 0.6 copy.16
  (4 shorter events, 0.0 us)
Async XLA Ops:
  6.5 67.1 %all-gather.13.cloned.1.call-start = ((), (), s32[]{:S(2)}) async-start(), calls=%async_computation.4 | async-start | bytes 1179648 | tf_op jit(solution)/shard_map/all_gather | solution.py:28
  7.3 148.0 %all-gather.11.cloned.1.call-start = ((), (), s32[]{:S(2)}) async-start(), calls=%async_computation.3 | async-start | bytes 4718592 | tf_op jit(solution)/shard_map/all_gather | solution.py:22
  8.0 219.8 %all-gather.7.cloned.1.call-start = ((), (), s32[]{:S(2)}) async-start(), calls=%async_computation.1 | async-start | bytes 4718592 | tf_op jit(solution)/shard_map/all_gather | solution.py:44
  36.0 18.6 %copy-start.1 = (s32[4,6]{1,0:T(4,128)S(1)}, s32[4,6]{1,0:T(4,128)}, u32[]{:S(2)}) copy-start(s32[4,6]{1,0:T(4,128)} %param.17) | copy-start | bytes 292
  47.2 81.2 %all-to-all-start = ((bf16[8,2,65536]{2,1,0:T(2,128)(2,1)}), bf16[8,2,65536]{2,1,0:T(2,128)(2,1)S(1)}, u32[]{:S(2)}, u32[]{:S(2)}) async-start(bf16[8,2,65536]{2,1,0:T(2,128)(2,1)} %reshape.112), calls=%async_computation | async-start | bytes 4194304 | tf_op jit(solution)/shard_map/all_to_all | solution.py:40
  54.5 213.1 %all-gather.9.cloned.1.call-start = ((), (), s32[]{:S(2)}) async-start(), calls=%async_computation.2 | async-start | bytes 1179648 | tf_op jit(solution)/shard_map/all_gather | solution.py:32
  267.6 45.8 %copy-start = (bf16[24,32,2048]{2,1,0:T(8,128)(2,1)S(1)}, bf16[24,32,2048]{2,1,0:T(8,128)(2,1)}, u32[]{:S(2)}) copy-start(bf16[24,32,2048]{2,1,0:T(8,128)(2,1)} %gather_fusion.1) | copy-start | bytes 9437188
Sparse Core Ops, SparseCore 0:
  9.4 42.1 all-gather.12
  53.7 100.0 all-gather.10
  156.0 71.7 all-gather.6
  229.7 37.9 all-gather.8
